TPU v7x, 512 devices: a whole 4x8x8 slice. The times are simulated.
512 devices in a mesh: side: 2 (over y_hi), grp: 8 (over z), dev: 32 (over x, y_lo, core).
Axes of the slice: x: 4, y: 8 (y_hi: 2, y_lo: 4; y = y_hi * 4 + y_lo), z: 8, core: 2. Of those that a mesh axis runs over, the one named last changes fastest.
Arguments:
- sources: float32 [2, 8, 65536], P('side', None, ('grp', 'dev')), may hold values from -2500 to 2500
- near_blocks: bfloat16 [2, 8192, 128, 128], P('side', ('grp', 'dev')), may hold values from -0.125 to 0.125
- block_rows: int32 [2, 8192], P('side', ('grp', 'dev')), may hold values from 0 to 1, as said below
- block_cols: int32 [2, 8192], P('side', ('grp', 'dev')), may hold values from 0 to 511, as said below
- mirror: int32 [65536], P(('grp', 'dev')), may hold values from 0 to 127, as said below
Outputs:
- krylov_basis: float32 [4, 2, 8, 65536], P(None, 'side', None, ('grp', 'dev'))
- hessenberg: float32 [8, 4, 3], replicated
Inputs may be any that keep to these rules, and one draw needn't show every extreme that they name: `block_rows`: in each device's aligned run of 32 entries, the first 2 are 0 to 1 in order. `block_cols`: in each device's aligned run of 32 entries, the first 2 name that device's own blocks in order, and every entry names a block of an owner at most 4 owners before or after that device (owners of a half counted in the order grp, dev); where such owners exist, some entry names a block of the owner 4 before and some one of the owner 4 after. `mirror`: each aligned run of 128 entries is a permutation of 0 to 127.
All inputs are finite; a program needn't handle non-finite values.
Results may differ from a plain program's by a relative error of at most 0.005.
Values may be sent and summed in bfloat16 or wider, within the bound.
A program may use at most 64 MiB of HBM per device.

v0:
```python
import jax
import jax.numpy as jnp
from jax import lax
from jax.sharding import PartitionSpec as P

BLOCK = 128
BLK_DEV = 2
WIN = 4
ITERS = 3
epsilon = 1e-06


def shifted(block, axis, distance):
    devices = range(lax.axis_size(axis))
    route = [(i - distance, i) for i in devices if i - distance in devices]
    return lax.ppermute(block, axis, route)


def swapped(value, axis, distance):
    return lax.ppermute(value, axis, [(i, i ^ 1 << distance) for i in range(lax.axis_size(axis))])


def on_device(sources, near_blocks, block_rows, block_cols, mirror):
    side_index = lax.axis_index("side")
    is_port = side_index == 0
    owner_index = lax.axis_index(("grp", "dev"))
    vectors = sources.shape[1]
    panels = sources.shape[2]
    total_panels = (
        1.0 * panels * lax.axis_size("side") * lax.axis_size("grp") * lax.axis_size("dev")
    )
    mirror_onehot = (
        mirror.reshape(BLK_DEV, BLOCK)[:, :, None]
        == jnp.arange(BLOCK, dtype=jnp.int32)[None, None, :]
    ).astype(jnp.float32)
    row_onehot = (block_rows[0][None, :] == jnp.arange(BLK_DEV, dtype=jnp.int32)[:, None]).astype(
        jnp.float32
    )
    window_cols = block_cols[0] - (owner_index - WIN) * BLK_DEV
    blocks = near_blocks[0]
    start = sources[0]
    inner_scale = 1.0 / total_panels
    squares = lax.psum(jnp.sum(start * start, axis=1), ("side", "grp", "dev"))
    length = jnp.sqrt(squares * inner_scale + epsilon)
    vectors_list = [start / length[:, None]]
    hessenberg = jnp.zeros((vectors, ITERS + 1, ITERS), jnp.float32)
    for column in range(ITERS):
        operator_vector = vectors_list[column]
        operator_partner = swapped(operator_vector, "side", 0)
        port_part = jnp.where(is_port, operator_vector, operator_partner)
        star_part = jnp.where(is_port, operator_partner, operator_vector)
        parity = jnp.where(is_port, 1.0, -1.0).astype(jnp.float32)
        mirrored_shaped = star_part.reshape(star_part.shape[:-1] + (BLK_DEV, BLOCK))
        field = port_part + parity * jnp.einsum(
            "bij,...bj->...bi", mirror_onehot, mirrored_shaped, precision=lax.Precision.HIGHEST
        ).reshape(star_part.shape)
        near_rounded = field.astype(jnp.bfloat16)
        below_list = []
        above_list = []
        for distance in range(1, WIN + 1):
            below_list.append(shifted(near_rounded, ("grp", "dev"), distance))
            above_list.append(shifted(near_rounded, ("grp", "dev"), -distance))
        window = jnp.concatenate(below_list[::-1] + [near_rounded] + above_list, axis=1)
        picked = window.reshape(vectors, -1, BLOCK)[:, window_cols]
        products = jnp.einsum("rkj,kij->rki", picked, blocks, preferred_element_type=jnp.float32)
        summed = jnp.einsum("bk,rki->rbi", row_onehot, products, precision=lax.Precision.HIGHEST)
        image = 0.5 * field + summed.reshape(vectors, panels)
        returned = swapped(image, "side", 0)
        symmetric = jnp.where(is_port, image, returned)
        antisym = jnp.where(is_port, returned, image)
        vector = 0.5 * (symmetric - antisym)
        shaped = vector.reshape(vector.shape[:-1] + (BLK_DEV, BLOCK))
        image = jnp.where(
            is_port,
            0.5 * (symmetric + antisym),
            jnp.einsum(
                "bij,...bi->...bj", mirror_onehot, shaped, precision=lax.Precision.HIGHEST
            ).reshape(vector.shape),
        )
        stacked = jnp.stack(vectors_list)
        products_local = jnp.sum(image[None] * stacked, axis=2)
        dot_sums = lax.psum(products_local, ("side", "grp", "dev"))
        coeffs = dot_sums * inner_scale
        remainder = image - jnp.einsum(
            "jr,jrp->rp", coeffs, stacked, precision=lax.Precision.HIGHEST
        )
        rem_squares = (
            lax.psum(jnp.sum(remainder * remainder, axis=1), ("side", "grp", "dev")) * inner_scale
        )
        rem_norm = jnp.sqrt(rem_squares + epsilon)
        vectors_list.append(remainder / rem_norm[:, None])
        hessenberg = hessenberg.at[:, : column + 1, column].set(coeffs.T)
        hessenberg = hessenberg.at[:, column + 1, column].set(rem_norm)
    final = jnp.stack(vectors_list)
    return (final[:, None], hessenberg)


def solution(mesh):
    placed = (
        P("side", None, ("grp", "dev")),
        P("side", ("grp", "dev"), None, None),
        P("side", ("grp", "dev")),
        P("side", ("grp", "dev")),
        P(("grp", "dev")),
    )
    return jax.shard_map(
        on_device,
        mesh=mesh,
        in_specs=placed,
        out_specs=(P(None, "side", None, ("grp", "dev")), P()),
        check_vma=False,
    )
```

profile of v0, /device:TPU:1, one launch (start us, length us, event | category | flops | bytes accessed | tf_op | source)
XLA Modules:
  0.0 840.6 jit_solution(13101358596570558061)
XLA Ops:
  1.6 106.1 %psum.49 = f32[8]{0:T(128)S(1)} all-reduce(f32[8]{0:T(128)S(1)} %fusion.35), channel_id=1, replica_groups=mesh['side'=2,'grp'=8,'dev'=32] {'side','grp','dev'}, use_global_device_ids=true, to_apply=%region_1.0 | all-reduce | flops 8 | bytes 64 | tf_op jit(solution)/shard_map/psum | solution.py:43
  107.8 4.7 collective-permute-start
  113.2 2.9 collective-permute-done
  116.3 2.6 collective-permute-start.1
  118.9 5.9 collective-permute-start.2
  124.8 2.4 collective-permute-start.3
  127.3 2.0 collective-permute-start.4
  129.2 2.3 collective-permute-start.5
  136.0 3.5 collective-permute-done.7
  143.0 5.2 collective-permute-start.9
  148.1 3.1 collective-permute-done.9
  151.6 104.0 %psum.50 = f32[1,8]{1,0:T(1,128)S(1)} all-reduce(f32[1,8]{1,0:T(1,128)S(1)} %bitcast.209), channel_id=1, replica_groups=mesh['side'=2,'grp'=8,'dev'=32] {'side','grp','dev'}, use_global_device_ids=true, to_apply=%region_3.4 | all-reduce | flops 8 | bytes 64 | tf_op jit(solution)/shard_map/psum | solution.py:82
  255.9 94.4 %psum.51 = f32[8]{0:T(128)S(1)} all-reduce(f32[8]{0:T(128)S(1)} %get-tuple-element.76), channel_id=1, replica_groups=mesh['side'=2,'grp'=8,'dev'=32] {'side','grp','dev'}, use_global_device_ids=true, to_apply=%region_5.6 | all-reduce | flops 8 | bytes 64 | tf_op jit(solution)/shard_map/psum | solution.py:88
  350.3 4.0 collective-permute-start.10
  354.4 4.3 collective-permute-done.10
  360.8 7.8 collective-permute-start.12
  368.6 2.7 collective-permute-start.13
  373.2 2.4 collective-permute-start.15
  380.0 3.5 collective-permute-done.17
  386.3 4.1 collective-permute-start.19
  390.4 4.2 collective-permute-done.19
  394.9 103.1 %psum.52 = f32[2,8]{1,0:T(2,128)S(1)} all-reduce(f32[2,8]{1,0:T(2,128)S(1)} %get-tuple-element.81), channel_id=1, replica_groups=mesh['side'=2,'grp'=8,'dev'=32] {'side','grp','dev'}, use_global_device_ids=true, to_apply=%region_7.8 | all-reduce | flops 16 | bytes 128 | tf_op jit(solution)/shard_map/psum | solution.py:82
  498.4 94.2 %psum.53 = f32[8]{0:T(128)S(1)} all-reduce(f32[8]{0:T(128)S(1)} %multiply_reduce_fusion.3), channel_id=1, replica_groups=mesh['side'=2,'grp'=8,'dev'=32] {'side','grp','dev'}, use_global_device_ids=true, to_apply=%region_9.10 | all-reduce | flops 8 | bytes 64 | tf_op jit(solution)/shard_map/psum | solution.py:88
  592.7 4.7 collective-permute-start.20
  598.0 3.0 collective-permute-done.20
  601.2 2.6 collective-permute-start.21
  603.8 7.1 collective-permute-start.22
  612.4 2.9 collective-permute-start.24
  621.6 4.0 collective-permute-done.27
  628.4 4.7 collective-permute-start.29
  637.1 104.3 %psum.54 = f32[3,8]{1,0:T(4,128)S(1)} all-reduce(f32[3,8]{1,0:T(4,128)S(1)} %get-tuple-element.79), channel_id=1, replica_groups=mesh['side'=2,'grp'=8,'dev'=32] {'side','grp','dev'}, use_global_device_ids=true, to_apply=%region_11.12 | all-reduce | flops 24 | bytes 192 | tf_op jit(solution)/shard_map/psum | solution.py:82
  741.8 94.4 %psum.55 = f32[8]{0:T(128)S(1)} all-reduce(f32[8]{0:T(128)S(1)} %multiply_reduce_fusion.2), channel_id=1, replica_groups=mesh['side'=2,'grp'=8,'dev'=32] {'side','grp','dev'}, use_global_device_ids=true, to_apply=%region_13.14 | all-reduce | flops 8 | bytes 64 | tf_op jit(solution)/shard_map/psum | solution.py:88
  (127 shorter events, 42.3 us)
Async XLA Ops:
  0.6 140.8 %copy-start = (bf16[1,32,128,128]{3,2,1,0:T(8,128)(2,1)S(1)}, bf16[1,32,128,128]{3,2,1,0:T(8,128)(2,1)}, u32[]{:S(2)}) copy-start(bf16[1,32,128,128]{3,2,1,0:T(8,128)(2,1)} %param.18) | copy-start | bytes 3145732
  0.6 107.1 %copy-start.1 = (f32[1,8,256]{2,1,0:T(8,128)S(1)}, f32[1,8,256]{2,1,0:T(8,128)}, u32[]{:S(2)}) copy-start(f32[1,8,256]{2,1,0:T(8,128)} %param.17) | copy-start | bytes 24580
  107.8 8.3 collective-permute-start
  116.3 15.2 %collective-permute-start.1 = (bf16[8,256]{1,0:T(8,128)(2,1)S(1)}, bf16[8,256]{1,0:T(8,128)(2,1)S(1)}, u32[]{:S(2)}, u32[]{:S(2)}) collective-permute-start(bf16[8,256]{1,0:T(8,128)(2,1)S(1)} %get-tuple-element.98), channel_id=1, source_target_pairs={{0,4},{1,5},{2,6},{3,7},{4,8},{5,9},{6,10},{7,11},{8,12},{9,13},{1... | collective-permute-start | bytes 12296 | tf_op jit(solution)/shard_map/ppermute | solution.py:16
  118.9 14.0 %collective-permute-start.2 = (bf16[8,256]{1,0:T(8,128)(2,1)S(1)}, bf16[8,256]{1,0:T(8,128)(2,1)S(1)}, u32[]{:S(2)}, u32[]{:S(2)}) collective-permute-start(bf16[8,256]{1,0:T(8,128)(2,1)S(1)} %get-tuple-element.98), channel_id=1, source_target_pairs={{0,3},{1,4},{2,5},{3,6},{4,7},{5,8},{6,9},{7,10},{8,11},{9,12},{10... | collective-permute-start | bytes 12296 | tf_op jit(solution)/shard_map/ppermute | solution.py:16
  124.8 9.4 %collective-permute-start.3 = (bf16[8,256]{1,0:T(8,128)(2,1)S(1)}, bf16[8,256]{1,0:T(8,128)(2,1)S(1)}, u32[]{:S(2)}, u32[]{:S(2)}) collective-permute-start(bf16[8,256]{1,0:T(8,128)(2,1)S(1)} %get-tuple-element.98), channel_id=1, source_target_pairs={{0,2},{1,3},{2,4},{3,5},{4,6},{5,7},{6,8},{7,9},{8,10},{9,11},{10,... | collective-permute-start | bytes 12296 | tf_op jit(solution)/shard_map/ppermute | solution.py:16
  127.3 8.3 collective-permute-start.4
  129.2 6.4 collective-permute-start.5
  131.6 4.4 collective-permute-start.6
  132.9 6.6 collective-permute-start.7
  134.2 6.6 collective-permute-start.8
  143.0 8.3 collective-permute-start.9
  350.3 8.3 collective-permute-start.10
  358.9 16.7 %collective-permute-start.11 = (bf16[8,256]{1,0:T(8,128)(2,1)S(1)}, bf16[8,256]{1,0:T(8,128)(2,1)S(1)}, u32[]{:S(2)}, u32[]{:S(2)}) collective-permute-start(bf16[8,256]{1,0:T(8,128)(2,1)S(1)} %get-tuple-element.102), channel_id=1, source_target_pairs={{0,4},{1,5},{2,6},{3,7},{4,8},{5,9},{6,10},{7,11},{8,12},{9,13},{1... | collective-permute-start | bytes 12296 | tf_op jit(solution)/shard_map/ppermute | solution.py:16
  360.8 16.2 %collective-permute-start.12 = (bf16[8,256]{1,0:T(8,128)(2,1)S(1)}, bf16[8,256]{1,0:T(8,128)(2,1)S(1)}, u32[]{:S(2)}, u32[]{:S(2)}) collective-permute-start(bf16[8,256]{1,0:T(8,128)(2,1)S(1)} %get-tuple-element.102), channel_id=1, source_target_pairs={{0,3},{1,4},{2,5},{3,6},{4,7},{5,8},{6,9},{7,10},{8,11},{9,12},{10... | collective-permute-start | bytes 12296 | tf_op jit(solution)/shard_map/ppermute | solution.py:16
  368.6 9.7 %collective-permute-start.13 = (bf16[8,256]{1,0:T(8,128)(2,1)S(1)}, bf16[8,256]{1,0:T(8,128)(2,1)S(1)}, u32[]{:S(2)}, u32[]{:S(2)}) collective-permute-start(bf16[8,256]{1,0:T(8,128)(2,1)S(1)} %get-tuple-element.102), channel_id=1, source_target_pairs={{0,2},{1,3},{2,4},{3,5},{4,6},{5,7},{6,8},{7,9},{8,10},{9,11},{10,... | collective-permute-start | bytes 12296 | tf_op jit(solution)/shard_map/ppermute | solution.py:16
  371.3 8.3 collective-permute-start.14
  373.2 6.4 collective-permute-start.15
  375.6 4.4 collective-permute-start.16
  377.0 6.5 collective-permute-start.17
  378.3 6.6 collective-permute-start.18
  386.3 8.3 collective-permute-start.19
  592.7 8.3 collective-permute-start.20
  601.2 16.1 %collective-permute-start.21 = (bf16[8,256]{1,0:T(8,128)(2,1)S(1)}, bf16[8,256]{1,0:T(8,128)(2,1)S(1)}, u32[]{:S(2)}, u32[]{:S(2)}) collective-permute-start(bf16[8,256]{1,0:T(8,128)(2,1)S(1)} %get-tuple-element.104), channel_id=1, source_target_pairs={{0,4},{1,5},{2,6},{3,7},{4,8},{5,9},{6,10},{7,11},{8,12},{9,13},{1... | collective-permute-start | bytes 12296 | tf_op jit(solution)/shard_map/ppermute | solution.py:16
  603.8 14.8 %collective-permute-start.22 = (bf16[8,256]{1,0:T(8,128)(2,1)S(1)}, bf16[8,256]{1,0:T(8,128)(2,1)S(1)}, u32[]{:S(2)}, u32[]{:S(2)}) collective-permute-start(bf16[8,256]{1,0:T(8,128)(2,1)S(1)} %get-tuple-element.104), channel_id=1, source_target_pairs={{0,3},{1,4},{2,5},{3,6},{4,7},{5,8},{6,9},{7,10},{8,11},{9,12},{10... | collective-permute-start | bytes 12296 | tf_op jit(solution)/shard_map/ppermute | solution.py:16
  610.9 9.0 %collective-permute-start.23 = (bf16[8,256]{1,0:T(8,128)(2,1)S(1)}, bf16[8,256]{1,0:T(8,128)(2,1)S(1)}, u32[]{:S(2)}, u32[]{:S(2)}) collective-permute-start(bf16[8,256]{1,0:T(8,128)(2,1)S(1)} %get-tuple-element.104), channel_id=1, source_target_pairs={{0,2},{1,3},{2,4},{3,5},{4,6},{5,7},{6,8},{7,9},{8,10},{9,11},{10,... | collective-permute-start | bytes 12296 | tf_op jit(solution)/shard_map/ppermute | solution.py:16
  612.4 8.8 %collective-permute-start.24 = (bf16[8,256]{1,0:T(8,128)(2,1)S(1)}, bf16[8,256]{1,0:T(8,128)(2,1)S(1)}, u32[]{:S(2)}, u32[]{:S(2)}) collective-permute-start(bf16[8,256]{1,0:T(8,128)(2,1)S(1)} %get-tuple-element.104), channel_id=1, source_target_pairs={{0,1},{1,2},{2,3},{3,4},{4,5},{5,6},{6,7},{7,8},{8,9},{9,10},{10,1... | collective-permute-start | bytes 12296 | tf_op jit(solution)/shard_map/ppermute | solution.py:16
  615.3 5.9 collective-permute-start.25
  617.3 4.4 collective-permute-start.26
  618.6 7.0 collective-permute-start.27
  619.9 7.1 collective-permute-start.28
  628.4 8.3 collective-permute-start.29
  (3 other events, 4.2 us)
where the time goes:
time: 842 us; the launch traced here: 841 us
  blocking collectives  700 us (83%)
  starting transfers between devices  86.9 us (10%)
  waiting for transfers between devices  34.7 us (4%)
    psum x3, blocking collectives, on_device(): dot_sums = lax.psum(products_local, ('side', 'grp', 'dev'))  311 us
    psum x3, blocking collectives, on_device(): lax.psum(jnp.sum(remainder * remainder, axis=1), ('side', 'grp', 'dev'))  283 us
    psum x1, blocking collectives, on_device(): squares = lax.psum(jnp.sum(start * start, axis=1), ('side', 'grp', 'dev'))  106 us
    ppermute x24, starting transfers between devices, shifted(): return lax.ppermute(block, axis, route)  59.5 us
    ppermute x6, starting transfers between devices, swapped(): lax.ppermute(value, axis, [(i, i ^ 1 << distance) for i in range(lax.axis...  27.3 us
    ppermute x6, waiting for transfers between devices, swapped(): lax.ppermute(value, axis, [(i, i ^ 1 << distance) for i in range(lax.axis...  18.5 us
  transfers between devices with their start and end apart: 30, of which 15 were waited for; matrix products, arithmetic and copies ran while one was open for 0% of the time, Pallas kernels for 0%

commit v1 on v0

--- a/solution.py
+++ b/solution.py
@@ -8,6 +8,11 @@
 WIN = 4
 ITERS = 3
 epsilon = 1e-06
+
+
+def one_after_other(value_2, inner_axis, outer_axis):
+    partial = lax.psum(value_2, inner_axis)
+    return lax.psum(partial, outer_axis)
 
 
 def shifted(block, axis, distance):
@@ -85,7 +90,8 @@
             "jr,jrp->rp", coeffs, stacked, precision=lax.Precision.HIGHEST
         )
         rem_squares = (
-            lax.psum(jnp.sum(remainder * remainder, axis=1), ("side", "grp", "dev")) * inner_scale
+            one_after_other(jnp.sum(remainder * remainder, axis=1), "side", ("grp", "dev"))
+            * inner_scale
         )
         rem_norm = jnp.sqrt(rem_squares + epsilon)
         vectors_list.append(remainder / rem_norm[:, None])

time: 842 us -> 2580 us (3.06)
  blocking collectives: 700 us -> 2450 us
    psum x3 -> x6, blocking collectives: 283 us -> 2020 us  [the longest x3 2000 us: one_after_other(): return lax.psum(partial, outer_axis)]
where the time goes in v1:
time: 2580 us
  blocking collectives  2450 us (95%)
  starting transfers between devices  74.5 us (3%)
  waiting for transfers between devices  34 us (1%)
    psum x3, blocking collectives, one_after_other(): return lax.psum(partial, outer_axis)  2000 us
    psum x3, blocking collectives, on_device(): dot_sums = lax.psum(products_local, ('side', 'grp', 'dev'))  327 us
    psum x1, blocking collectives, on_device(): squares = lax.psum(jnp.sum(start * start, axis=1), ('side', 'grp', 'dev'))  106 us
  transfers between devices with their start and end apart: 30, of which 15 were waited for; matrix products, arithmetic and copies ran while one was open for 0% of the time, Pallas kernels for 0%

profile of v1, /device:TPU:1, one launch (start us, length us, event | category | flops | bytes accessed | tf_op | source)
XLA Modules:
  0.0 2581.3 jit_solution(6570950832294002115)
XLA Ops:
  1.6 106.1 %psum.70 = f32[8]{0:T(128)S(1)} all-reduce(f32[8]{0:T(128)S(1)} %fusion.35), channel_id=1, replica_groups=mesh['side'=2,'grp'=8,'dev'=32] {'side','grp','dev'}, use_global_device_ids=true, to_apply=%region_1.0 | all-reduce | flops 8 | bytes 64 | tf_op jit(solution)/shard_map/psum | solution.py:48
  107.8 4.7 collective-permute-start
  113.2 2.9 collective-permute-done
  116.3 2.6 collective-permute-start.1
  118.9 5.9 collective-permute-start.2
  124.8 2.4 collective-permute-start.3
  127.3 2.0 collective-permute-start.4
  129.2 2.3 collective-permute-start.5
  136.0 3.5 collective-permute-done.7
  143.0 5.2 collective-permute-start.9
  148.1 3.1 collective-permute-done.9
  151.6 104.0 %psum.71 = f32[1,8]{1,0:T(1,128)S(1)} all-reduce(f32[1,8]{1,0:T(1,128)S(1)} %bitcast.209), channel_id=1, replica_groups=mesh['side'=2,'grp'=8,'dev'=32] {'side','grp','dev'}, use_global_device_ids=true, to_apply=%region_3.4 | all-reduce | flops 8 | bytes 64 | tf_op jit(solution)/shard_map/psum | solution.py:87
  255.9 7.7 psum.72
  263.6 666.1 %psum.73 = f32[8]{0:T(128)S(1)} all-reduce(f32[8]{0:T(128)S(1)} %psum.72), channel_id=1, replica_groups=mesh['side'=2,'grp'=8,'dev'=32] {'grp','dev'}, use_global_device_ids=true, to_apply=%region_6.7 | all-reduce | flops 8 | bytes 64 | tf_op jit(solution)/shard_map/psum | solution.py:15
  929.7 4.2 collective-permute-start.10
  934.0 4.0 collective-permute-done.10
  944.1 3.7 collective-permute-start.15
  952.4 2.7 collective-permute-done.17
  958.3 5.0 collective-permute-start.19
  963.3 3.3 collective-permute-done.19
  967.0 110.7 %psum.74 = f32[2,8]{1,0:T(2,128)S(1)} all-reduce(f32[2,8]{1,0:T(2,128)S(1)} %get-tuple-element.81), channel_id=1, replica_groups=mesh['side'=2,'grp'=8,'dev'=32] {'side','grp','dev'}, use_global_device_ids=true, to_apply=%region_8.9 | all-reduce | flops 16 | bytes 128 | tf_op jit(solution)/shard_map/psum | solution.py:87
  1078.0 7.7 psum.75
  1085.7 666.1 %psum.76 = f32[8]{0:T(128)S(1)} all-reduce(f32[8]{0:T(128)S(1)} %psum.75), channel_id=1, replica_groups=mesh['side'=2,'grp'=8,'dev'=32] {'grp','dev'}, use_global_device_ids=true, to_apply=%region_11.12 | all-reduce | flops 8 | bytes 64 | tf_op jit(solution)/shard_map/psum | solution.py:15
  1751.9 4.8 collective-permute-start.20
  1757.3 2.9 collective-permute-done.20
  1766.3 4.0 collective-permute-start.25
  1774.8 2.7 collective-permute-done.27
  1780.7 4.4 collective-permute-start.29
  1786.6 2.4 collective-permute-done.29
  1789.4 111.8 %psum.77 = f32[3,8]{1,0:T(4,128)S(1)} all-reduce(f32[3,8]{1,0:T(4,128)S(1)} %get-tuple-element.79), channel_id=1, replica_groups=mesh['side'=2,'grp'=8,'dev'=32] {'side','grp','dev'}, use_global_device_ids=true, to_apply=%region_13.14 | all-reduce | flops 24 | bytes 192 | tf_op jit(solution)/shard_map/psum | solution.py:87
  1902.9 7.7 psum.78
  1910.7 666.1 %psum.79 = f32[8]{0:T(128)S(1)} all-reduce(f32[8]{0:T(128)S(1)} %psum.78), channel_id=1, replica_groups=mesh['side'=2,'grp'=8,'dev'=32] {'grp','dev'}, use_global_device_ids=true, to_apply=%region_16.17 | all-reduce | flops 8 | bytes 64 | tf_op jit(solution)/shard_map/psum | solution.py:15
  (130 shorter events, 47.2 us)
Async XLA Ops:
  0.6 140.8 %copy-start = (bf16[1,32,128,128]{3,2,1,0:T(8,128)(2,1)S(1)}, bf16[1,32,128,128]{3,2,1,0:T(8,128)(2,1)}, u32[]{:S(2)}) copy-start(bf16[1,32,128,128]{3,2,1,0:T(8,128)(2,1)} %param.18) | copy-start | bytes 3145732
  0.6 107.1 %copy-start.1 = (f32[1,8,256]{2,1,0:T(8,128)S(1)}, f32[1,8,256]{2,1,0:T(8,128)}, u32[]{:S(2)}) copy-start(f32[1,8,256]{2,1,0:T(8,128)} %param.17) | copy-start | bytes 24580
  107.8 8.3 collective-permute-start
  116.3 15.2 collective-permute-start.1
  118.9 14.0 collective-permute-start.2
  124.8 9.4 collective-permute-start.3
  127.3 8.3 collective-permute-start.4
  129.2 6.4 collective-permute-start.5
  131.6 4.4 collective-permute-start.6
  132.9 6.6 collective-permute-start.7
  134.2 6.6 collective-permute-start.8
  143.0 8.3 collective-permute-start.9
  929.7 8.3 collective-permute-start.10
  938.3 9.6 collective-permute-start.11
  939.6 9.6 collective-permute-start.12
  940.9 9.6 collective-permute-start.13
  942.2 9.7 collective-permute-start.14
  944.1 7.8 collective-permute-start.15
  947.9 4.5 collective-permute-start.16
  949.2 5.8 collective-permute-start.17
  950.5 6.3 collective-permute-start.18
  958.3 8.3 collective-permute-start.19
  1751.9 8.3 collective-permute-start.20
  1760.5 9.8 collective-permute-start.21
  1761.8 9.8 collective-permute-start.22
  1763.1 9.9 collective-permute-start.23
  1764.4 9.9 collective-permute-start.24
  1766.3 8.0 collective-permute-start.25
  1770.3 4.5 collective-permute-start.26
  1771.6 5.8 collective-permute-start.27
  1772.9 6.3 collective-permute-start.28
  1780.7 8.3 collective-permute-start.29
  (3 other events, 4.2 us)
